TPU v7x, 512 devices: a whole 4x4x16 slice. The times are simulated.
512 devices in a mesh: dp: 16 (over y, z_hi), seq: 32 (over z_lo, x, core).
Axes of the slice: x: 4, y: 4, z: 16 (z_hi: 4, z_lo: 4; z = z_hi * 4 + z_lo), core: 2. Of those that a mesh axis runs over, the one named last changes fastest.
Arguments:
- tokens: bfloat16 [1024, 64, 1152], P(('dp', 'seq')), may hold values from -6 to 6
- spatial_qkv: bfloat16 [1024, 64, 1728], P(('dp', 'seq')), may hold values from -6 to 6
- wo_spatial: bfloat16 [576, 1152], replicated, may hold values from -0.25 to 0.25
- w_temporal: bfloat16 [1152, 1728], P(None, 'dp'), may hold values from -0.1875 to 0.1875
- wo_temporal: bfloat16 [576, 1152], replicated, may hold values from -0.25 to 0.25
- cotangent: bfloat16 [1024, 64, 1152], P(('dp', 'seq')), may hold values from -24 to 24
Outputs:
- block_out: bfloat16 [1024, 64, 1152], P(('dp', 'seq'))
- tokens_grad: bfloat16 [1024, 64, 1152], P(('dp', 'seq'))
- spatial_qkv_grad: bfloat16 [1024, 64, 1728], P(('dp', 'seq'))
- wo_spatial_grad: float32 [576, 1152], P('seq', 'dp')
- wo_temporal_grad: float32 [576, 1152], P('seq', 'dp')
All inputs are finite; a program needn't handle non-finite values.
Results may differ from a plain program's by a relative error of at most 0.038.
Values may be sent and summed in bfloat16 or wider, within the bound.
A program may use at most 64 MiB of HBM per device.

v0:
```python
import math
import jax
import jax.numpy as jnp
from jax import lax
from jax.sharding import PartitionSpec as P

DH = 72
FRAMES = 16


def split_three(packed):
    inner_width = packed.shape[-1] // 3
    return (
        packed[..., :inner_width],
        packed[..., inner_width : 2 * inner_width],
        packed[..., 2 * inner_width :],
    )


def head_view(matrix):
    batch_size, length, inner_width = matrix.shape
    return matrix.reshape(batch_size, length, inner_width // DH, DH)


def attention_weights_of(query_heads, key_heads):
    scores = jnp.einsum(
        "blhd,bmhd->bhlm", query_heads, key_heads, preferred_element_type=jnp.float32
    ) * (1.0 / math.sqrt(DH))
    return jax.nn.softmax(scores, axis=-1)


def attention(queries, key_rows, values):
    batch_size, length, inner_width = queries.shape
    weights_full = attention_weights_of(head_view(queries), head_view(key_rows))
    rounded = weights_full.astype(jnp.bfloat16)
    output = jnp.einsum(
        "bhlm,bmhd->blhd", rounded, head_view(values), preferred_element_type=jnp.float32
    )
    return output.reshape(batch_size, length, inner_width).astype(jnp.bfloat16)


def attention_grad(queries, key_rows, values, output_grad):
    batch_size, length, inner_width = queries.shape
    query_heads = head_view(queries)
    key_heads = head_view(key_rows)
    value_heads = head_view(values)
    grad_heads = head_view(output_grad)
    weights_full = attention_weights_of(query_heads, key_heads)
    rounded = weights_full.astype(jnp.bfloat16)
    value_grad = jnp.einsum(
        "bhlm,blhd->bmhd", rounded, grad_heads, preferred_element_type=jnp.float32
    )
    weight_grad = jnp.einsum(
        "blhd,bmhd->bhlm", grad_heads, value_heads, preferred_element_type=jnp.float32
    )
    centered = weight_grad - jnp.sum(weights_full * weight_grad, axis=-1, keepdims=True)
    score_grad = (weights_full * centered * (1.0 / math.sqrt(DH))).astype(jnp.bfloat16)
    query_grad = jnp.einsum(
        "bhlm,bmhd->blhd", score_grad, key_heads, preferred_element_type=jnp.float32
    )
    key_grad = jnp.einsum(
        "bhlm,blhd->bmhd", score_grad, query_heads, preferred_element_type=jnp.float32
    )
    joined = [
        part_grad.reshape(batch_size, length, inner_width)
        for part_grad in (query_grad, key_grad, value_grad)
    ]
    return jnp.concatenate(joined, axis=-1).astype(jnp.bfloat16)


def to_clips(matrix, clip_count):
    frame_total, patch_share, channels = matrix.shape
    grouped = matrix.reshape(clip_count, FRAMES, patch_share, channels).transpose(0, 2, 1, 3)
    return grouped.reshape(clip_count * patch_share, FRAMES, channels)


def from_clips(matrix, clip_count):
    batch_rows, frame_count, channels = matrix.shape
    patch_share = batch_rows // clip_count
    grouped = matrix.reshape(clip_count, patch_share, frame_count, channels).transpose(0, 2, 1, 3)
    return grouped.reshape(clip_count * frame_count, patch_share, channels)


def times_transposed(left, right):
    return lax.dot_general(
        left, right, (((1,), (1,)), ((), ())), preferred_element_type=jnp.float32
    )


def transposed_times(left, right):
    return lax.dot_general(
        left, right, (((0,), (0,)), ((), ())), preferred_element_type=jnp.float32
    )


def forward_project(hidden_rows, weight_shard):
    return jnp.dot(
        hidden_rows,
        lax.all_gather(weight_shard, "dp", axis=1, tiled=True),
        preferred_element_type=jnp.float32,
    )


def backward_project(grad_rows, weight_shard):
    return times_transposed(grad_rows, lax.all_gather(weight_shard, "dp", axis=1, tiled=True))


def shards(tokens, spatial_qkv, wo_spatial, w_temporal, wo_temporal, cotangent):
    frames_dev, patches, feature_width = tokens.shape
    row_total = frames_dev * patches
    seq_devices = lax.axis_size("seq")
    clip_count = frames_dev * seq_devices // FRAMES
    spatial_query, spatial_keys, spatial_values = split_three(spatial_qkv)
    spatial_out = attention(spatial_query, spatial_keys, spatial_values)
    spatial_rows = spatial_out.reshape(row_total, -1)
    hidden_rows = (
        tokens.reshape(row_total, feature_width).astype(jnp.float32)
        + jnp.dot(spatial_rows, wo_spatial, preferred_element_type=jnp.float32)
    ).astype(jnp.bfloat16)
    frame_qkv = (
        forward_project(hidden_rows, w_temporal)
        .astype(jnp.bfloat16)
        .reshape(frames_dev, patches, -1)
    )
    patch_qkv = lax.all_to_all(frame_qkv, "seq", split_axis=1, concat_axis=0, tiled=True)
    temporal_query, temporal_keys, temporal_values = split_three(to_clips(patch_qkv, clip_count))
    patch_out = from_clips(attention(temporal_query, temporal_keys, temporal_values), clip_count)
    temporal_out = lax.all_to_all(patch_out, "seq", split_axis=0, concat_axis=1, tiled=True)
    temporal_rows = temporal_out.reshape(row_total, -1)
    block_out = (
        hidden_rows.astype(jnp.float32)
        + jnp.dot(temporal_rows, wo_temporal, preferred_element_type=jnp.float32)
    ).astype(jnp.bfloat16)
    grad_rows = cotangent.reshape(row_total, feature_width)
    out_grad = (
        times_transposed(grad_rows, wo_temporal)
        .astype(jnp.bfloat16)
        .reshape(frames_dev, patches, -1)
    )
    temporal_part = transposed_times(temporal_rows, grad_rows).astype(jnp.bfloat16)
    patch_out_grad = lax.all_to_all(out_grad, "seq", split_axis=1, concat_axis=0, tiled=True)
    clip_qkv_grad = attention_grad(
        temporal_query, temporal_keys, temporal_values, to_clips(patch_out_grad, clip_count)
    )
    patch_qkv_grad = from_clips(clip_qkv_grad, clip_count)
    frame_qkv_grad = lax.all_to_all(patch_qkv_grad, "seq", split_axis=0, concat_axis=1, tiled=True)
    projection_grad = backward_project(frame_qkv_grad.reshape(row_total, -1), w_temporal).astype(
        jnp.bfloat16
    )
    tokens_grad = (grad_rows.astype(jnp.float32) + projection_grad.astype(jnp.float32)).astype(
        jnp.bfloat16
    )
    spatial_out_grad = (
        times_transposed(tokens_grad, wo_spatial)
        .astype(jnp.bfloat16)
        .reshape(frames_dev, patches, -1)
    )
    spatial_part = transposed_times(spatial_rows, tokens_grad).astype(jnp.bfloat16)
    spatial_qkv_grad = attention_grad(spatial_query, spatial_keys, spatial_values, spatial_out_grad)
    seq_sums = (
        lax.psum_scatter(spatial_part, "seq", scatter_dimension=0, tiled=True).astype(jnp.float32),
        lax.psum_scatter(temporal_part, "seq", scatter_dimension=0, tiled=True).astype(jnp.float32),
    )
    spatial_weight_grad, temporal_weight_grad = (
        lax.psum_scatter(
            seq_sums[0].astype(jnp.bfloat16), "dp", scatter_dimension=1, tiled=True
        ).astype(jnp.float32),
        lax.psum_scatter(
            seq_sums[1].astype(jnp.bfloat16), "dp", scatter_dimension=1, tiled=True
        ).astype(jnp.float32),
    )
    return (
        block_out.reshape(frames_dev, patches, feature_width),
        tokens_grad.reshape(frames_dev, patches, feature_width),
        spatial_qkv_grad,
        spatial_weight_grad,
        temporal_weight_grad,
    )


def solution(mesh):
    placed = (
        P(("dp", "seq"), None, None),
        P(("dp", "seq"), None, None),
        P(),
        P(None, "dp"),
        P(),
        P(("dp", "seq"), None, None),
    )
    return jax.shard_map(
        shards,
        mesh=mesh,
        in_specs=placed,
        out_specs=(
            P(("dp", "seq"), None, None),
            P(("dp", "seq"), None, None),
            P(("dp", "seq"), None, None),
            P("seq", "dp"),
            P("seq", "dp"),
        ),
        check_vma=False,
    )
```

profile of v0, /device:TPU:2, one launch (start us, length us, event | category | flops | bytes accessed | tf_op | source)
XLA Modules:
  0.0 741.1 jit_solution(11731465842137330203)
XLA Ops:
  7.2 0.7 all-gather.3.cloned.1.call-update
  7.9 0.6 copy-done
  8.5 1.5 convolution_convert_fusion.13
  10.2 0.8 copy.76
  11.0 10.1 %all-to-all-start.2 = ((bf16[2,64,576]{2,0,1:T(2,128)(2,1)}), bf16[2,64,576]{2,0,1:T(2,128)(2,1)}, u32[]{:S(2)}, u32[]{:S(2)}) async-start(bf16[2,64,576]{2,0,1:T(2,128)(2,1)} %copy.76), calls=%async_computation.2 | async-start | bytes 327680 | tf_op jit(solution)/shard_map/all_to_all | solution.py:141
  22.1 1.2 fusion.123
  23.3 2.4 fusion.21
  25.7 1.1 copy.62
  27.0 0.4 fusion.7
  27.4 121.9 %all-gather.3.cloned.1.call-done = bf16[16,108,1152]{2,1,0:T(8,128)(2,1)} async-done(((bf16[1,108,1152]{2,1,0:T(8,128)(2,1)}), bf16[16,108,1152]{2,1,0:T(8,128)(2,1)}) %all-gather.3.cloned.1.call-update) | async-done | bytes 3981328 | tf_op jit(solution)/shard_map/all_gather | solution.py:99
  149.4 4.8 reshape.139
  154.2 4.1 convolution_convert_fusion.3
  158.3 1.2 copy.63
  159.5 1.2 copy.64
  160.8 5.0 all-to-all-start
  165.7 1.0 copy.77
  166.8 0.7 copy.78
  167.5 1.9 reshape_reshape.6
  169.4 9.7 %all-to-all-done = bf16[2,64,1728]{2,0,1:T(2,128)(2,1)S(1)} async-done(((bf16[2,64,1728]{2,0,1:T(2,128)(2,1)}), bf16[2,64,1728]{2,0,1:T(2,128)(2,1)S(1)}, u32[]{:S(2)}, u32[]{:S(2)}) %all-to-all-start) | async-done | bytes 442400 | tf_op jit(solution)/shard_map/all_to_all | solution.py:125
  179.0 0.4 copy.65
  179.5 0.8 fusion.121
  180.2 1.9 reshape.123
  182.1 1.0 reshape.124
  183.1 1.2 reshape.122
  184.3 1.1 fusion.42
  185.4 2.2 fusion.128
  187.6 2.3 fusion.22
  189.9 1.0 copy.71
  190.9 0.9 convert_element_type.101
  191.8 0.9 copy.72
  192.7 0.8 copy.73
  193.5 5.9 all-to-all-start.1
  199.4 2.2 fusion.25
  201.6 1.0 copy.87
  202.6 0.9 concatenate.17
  203.5 1.9 fusion.24
  205.5 0.9 concatenate.16
  206.3 2.0 fusion.23
  208.4 0.9 concatenate.15
  209.3 1.2 concatenate.18
  210.6 1.2 copy.89
  211.8 8.0 %all-to-all-start.3 = ((bf16[64,2,1728]{2,1,0:T(2,128)(2,1)}), bf16[64,2,1728]{2,1,0:T(2,128)(2,1)}, u32[]{:S(2)}, u32[]{:S(2)}) async-start(bf16[64,2,1728]{2,1,0:T(2,128)(2,1)} %copy.89), calls=%async_computation.3 | async-start | bytes 917504 | tf_op jit(solution)/shard_map/all_to_all | solution.py:146
  219.8 1.7 copy.198
  221.5 1.0 reshape.126
  222.6 1.6 convolution_convert_fusion
  224.2 8.9 %all-to-all-done.3 = bf16[64,2,1728]{2,1,0:T(2,128)(2,1)} async-done(((bf16[64,2,1728]{2,1,0:T(2,128)(2,1)}), bf16[64,2,1728]{2,1,0:T(2,128)(2,1)}, u32[]{:S(2)}, u32[]{:S(2)}) %all-to-all-start.3) | async-done | bytes 442400 | tf_op jit(solution)/shard_map/all_to_all | solution.py:146
  233.1 2.1 copy.197
  235.2 2.2 reshape.132
  237.4 3.1 fusion.6
  240.5 1.6 convolution_convert_fusion.1
  242.2 1.3 dynamic-slice.2
  243.5 1.3 dynamic-slice
  246.1 1.1 fusion.8
  247.2 0.5 convolution_convert_fusion.12
  248.4 0.3 copy-done.16
  248.7 1.7 fusion.26
  250.4 0.4 fusion.28
  250.8 275.0 %all-reduce.9.cloned.1.call-done = (bf16[576,1152]{1,0:T(8,128)(2,1)}, bf16[576,1152]{1,0:T(8,128)(2,1)}) async-done(((bf16[576,1152]{1,0:T(8,128)(2,1)}, bf16[576,1152]{1,0:T(8,128)(2,1)}), (bf16[576,1152]{1,0:T(8,128)(2,1)}, bf16[576,1152]{1,0:T(8,128)(2,1)})) %all-reduce.9.cloned.1.call-update) | async-done | bytes 2654224
  525.8 1.6 constant_dynamic-slice_fusion
  527.4 1.6 fusion.27
  530.2 1.0 concatenate.19
  531.1 200.7 %all-reduce.11.cloned.1.call-done = (bf16[18,1152]{1,0:T(8,128)(2,1)}, bf16[18,1152]{1,0:T(8,128)(2,1)}) async-done(((bf16[18,1152]{1,0:T(8,128)(2,1)}, bf16[18,1152]{1,0:T(8,128)(2,1)}), (bf16[18,1152]{1,0:T(8,128)(2,1)}, bf16[18,1152]{1,0:T(8,128)(2,1)})) %all-reduce.11.cloned.1.call-update) | async-done | bytes 82960
  731.8 1.4 dynamic-slice_convert_fusion.1
  733.2 1.4 dynamic-slice_convert_fusion
  (58 shorter events, 3.5 us)
Async XLA Ops:
  7.2 1.3 copy-start
  7.2 142.2 %all-gather.3.cloned.1.call-start = ((), (), s32[]{:S(2)}) async-start(), calls=%async_computation.4 | async-start | bytes 4386816 | tf_op jit(solution)/shard_map/all_gather | solution.py:99
  8.5 12.6 %copy-start.11 = (bf16[2,64,1728]{2,1,0:T(8,128)(2,1)S(1)}, bf16[2,64,1728]{2,1,0:T(8,128)(2,1)}, u32[]{:S(2)}) copy-start(bf16[2,64,1728]{2,1,0:T(8,128)(2,1)} %param.7) | copy-start | bytes 1327108
  11.0 149.7 %all-to-all-start.2 = ((bf16[2,64,576]{2,0,1:T(2,128)(2,1)}), bf16[2,64,576]{2,0,1:T(2,128)(2,1)}, u32[]{:S(2)}, u32[]{:S(2)}) async-start(bf16[2,64,576]{2,0,1:T(2,128)(2,1)} %copy.76), calls=%async_computation.2 | async-start | bytes 327680 | tf_op jit(solution)/shard_map/all_to_all | solution.py:141
  21.5 1.8 copy-start.13
  21.8 1.5 copy-start.15
  22.1 1.2 copy-start.8
  23.3 3.7 copy-start.1
  23.3 3.7 copy-start.12
  27.0 127.2 %copy-start.4 = (bf16[128,576]{1,0:T(8,128)(2,1)}, bf16[128,576]{1,0:T(8,128)(2,1)S(1)}, u32[]{:S(2)}) copy-start(bf16[128,576]{1,0:T(8,128)(2,1)S(1)} %convert_element_type.94) | copy-start | bytes 442372
  160.8 18.3 %all-to-all-start = ((bf16[2,64,1728]{2,0,1:T(2,128)(2,1)}), bf16[2,64,1728]{2,0,1:T(2,128)(2,1)S(1)}, u32[]{:S(2)}, u32[]{:S(2)}) async-start(bf16[2,64,1728]{2,0,1:T(2,128)(2,1)} %copy.64), calls=%async_computation | async-start | bytes 917504 | tf_op jit(solution)/shard_map/all_to_all | solution.py:125
  179.5 4.9 copy-start.10
  193.5 18.3 %all-to-all-start.1 = ((bf16[64,2,576]{2,1,0:T(2,128)(2,1)}), bf16[64,2,576]{2,1,0:T(2,128)(2,1)}, u32[]{:S(2)}, u32[]{:S(2)}) async-start(bf16[64,2,576]{2,1,0:T(2,128)(2,1)} %copy.73), calls=%async_computation.1 | async-start | bytes 327680 | tf_op jit(solution)/shard_map/all_to_all | solution.py:128
  210.6 12.0 %copy-start.2 = (bf16[2,64,1152]{2,1,0:T(8,128)(2,1)S(1)}, bf16[2,64,1152]{2,1,0:T(8,128)(2,1)}, u32[]{:S(2)}) copy-start(bf16[2,64,1152]{2,1,0:T(8,128)(2,1)} %param.11) | copy-start | bytes 884740
  211.8 21.3 %all-to-all-start.3 = ((bf16[64,2,1728]{2,1,0:T(2,128)(2,1)}), bf16[64,2,1728]{2,1,0:T(2,128)(2,1)}, u32[]{:S(2)}, u32[]{:S(2)}) async-start(bf16[64,2,1728]{2,1,0:T(2,128)(2,1)} %copy.89), calls=%async_computation.3 | async-start | bytes 917504 | tf_op jit(solution)/shard_map/all_to_all | solution.py:146
  219.8 306.0 %all-reduce.9.cloned.1.call-start = ((), (), s32[]{:S(2)}) async-start(), calls=%async_computation.5 | async-start | bytes 5308416
  222.6 12.7 %copy-start.6 = (bf16[128,576]{1,0:T(8,128)(2,1)}, bf16[128,576]{1,0:T(8,128)(2,1)S(1)}, u32[]{:S(2)}) copy-start(bf16[128,576]{1,0:T(8,128)(2,1)S(1)} %reshape.126) | copy-start | bytes 442372
  237.4 3.1 copy-start.5
  240.5 6.7 copy-start.3
  242.1 3.9 copy-start.7
  242.2 489.6 %all-reduce.11.cloned.1.call-start = ((), (), s32[]{:S(2)}) async-start(), calls=%async_computation.6 | async-start | bytes 221184
  247.2 1.0 copy-start.9
  247.7 1.0 copy-start.16
  248.7 1.7 copy-start.14
Sparse Core Ops, SparseCore 0:
  11.1 138.2 all-gather.2
  242.3 283.4 all-reduce.8
  528.8 202.9 all-reduce.10
where the time goes:
time: 742 us; the launch traced here: 741 us
  waiting for transfers between devices  617 us (83%)
  local copies, waits for them, and re-layouts  43.8 us (6%)
  matrix products  33.1 us (4%)
  starting transfers between devices  29 us (4%)
  between operations  15.5 us (2%)
    unnamed x5, waiting for transfers between devices  476 us
    all_gather x1, waiting for transfers between devices, forward_project(): lax.all_gather(weight_shard, 'dp', axis=1, tiled=True)  122 us
  transfers between devices with their start and end apart: 7, of which 5 were waited for; matrix products, arithmetic and copies ran while one was open for 7% of the time, Pallas kernels for 0%

commit v1 on v0

--- a/solution.py
+++ b/solution.py
@@ -94,11 +94,13 @@
 
 
 def forward_project(hidden_rows, weight_shard):
-    return jnp.dot(
-        hidden_rows,
-        lax.all_gather(weight_shard, "dp", axis=1, tiled=True),
-        preferred_element_type=jnp.float32,
-    )
+
+    def _register_joints(view):
+        z1 = jnp.stack([view] * lax.axis_size("dp"))
+        low = jnp.concatenate(lax.all_to_all(z1, "dp", 0, 0), axis=1)
+        return low
+
+    return jnp.dot(hidden_rows, _register_joints(weight_shard), preferred_element_type=jnp.float32)
 
 
 def backward_project(grad_rows, weight_shard):

time: 742 us -> 886 us (1.19)
  waiting for transfers between devices: 617 us -> 726 us
  starting transfers between devices: 29 us -> 47.9 us
  local copies, waits for them, and re-layouts: 43.8 us -> 58.7 us
    all_to_all x0 -> x1, waiting for transfers between devices: none -> 198 us  [_register_joints(): low = jnp.concatenate(lax.all_to_all(z1, 'dp', 0, 0), axis=1)]
    all_gather x1, waiting for transfers between devices: 122 us -> 0.02 us  [backward_project(): lax.all_gather(weight_shard, 'dp', axis=1, tiled=True)]
    all_to_all x1, waiting for transfers between devices: 9.68 us -> 42 us  [shards(): lax.all_to_all(frame_qkv, 'seq', split_axis=1, concat_axis=0, tiled=True)]
    all_to_all x0 -> x1, starting transfers between devices: none -> 18 us  [_register_joints(): low = jnp.concatenate(lax.all_to_all(z1, 'dp', 0, 0), axis=1)]
  transfers between devices with their start and end apart: 7 -> 8, of which waited for: 5 -> 5; matrix products, arithmetic and copies ran while one was open for 7% -> 9% of each run, Pallas kernels for 0% -> 0%
where the time goes in v1:
time: 886 us; the launch traced here: 884 us
  waiting for transfers between devices  726 us (82%)
  local copies, waits for them, and re-layouts  58.7 us (7%)
  starting transfers between devices  47.9 us (5%)
  matrix products  33.4 us (4%)
  between operations  15.4 us (2%)
    unnamed x5, waiting for transfers between devices  483 us
    all_to_all x1, waiting for transfers between devices, _register_joints(): low = jnp.concatenate(lax.all_to_all(z1, 'dp', 0, 0), axis=1)  198 us
    all_to_all x1, waiting for transfers between devices, shards(): lax.all_to_all(frame_qkv, 'seq', split_axis=1, concat_axis=0, tiled=True)  42 us
    all_to_all x1, starting transfers between devices, _register_joints(): low = jnp.concatenate(lax.all_to_all(z1, 'dp', 0, 0), axis=1)  18 us
  transfers between devices with their start and end apart: 8, of which 5 were waited for; matrix products, arithmetic and copies ran while one was open for 9% of the time, Pallas kernels for 0%

profile of v1, /device:TPU:2, one launch (start us, length us, event | category | flops | bytes accessed | tf_op | source)
XLA Modules:
  0.0 884.5 jit_solution(16105180142501121069)
XLA Ops:
  7.2 3.4 stack.2
  10.6 18.0 %all-to-all-start = ((bf16[16,1152,108]{1,2,0:T(8,128)(2,1)}), bf16[16,1152,108]{1,2,0:T(8,128)(2,1)}, u32[]{:S(2)}, u32[]{:S(2)}) async-start(bf16[16,1152,108]{1,2,0:T(8,128)(2,1)} %stack.2), calls=%async_computation | async-start | bytes 8257536 | tf_op jit(solution)/shard_map/all_to_all | solution.py:100
  28.7 0.7 all-gather.3.cloned.1.call-update
  30.3 1.1 fusion.123
  32.4 0.5 convolution_convert_fusion.13
  33.1 0.8 copy.77
  33.9 197.8 %all-to-all-done = bf16[16,1152,108]{1,2,0:T(8,128)(2,1)} async-done(((bf16[16,1152,108]{1,2,0:T(8,128)(2,1)}), bf16[16,1152,108]{1,2,0:T(8,128)(2,1)}, u32[]{:S(2)}, u32[]{:S(2)}) %all-to-all-start) | async-done | bytes 3981344 | tf_op jit(solution)/shard_map/all_to_all | solution.py:100
  231.8 7.2 all-to-all-start.3
  238.9 1.4 fusion.7
  240.3 5.1 reshape.128
  245.4 4.1 convolution_convert_fusion.3
  249.5 2.0 copy.64
  251.5 2.3 copy.65
  253.8 7.9 all-to-all-start.1
  261.7 1.0 copy.78
  262.7 0.7 copy.79
  263.4 1.9 reshape_reshape.6
  265.3 42.0 %all-to-all-done.1 = bf16[2,64,1728]{2,0,1:T(2,128)(2,1)} async-done(((bf16[2,64,1728]{2,0,1:T(2,128)(2,1)}), bf16[2,64,1728]{2,0,1:T(2,128)(2,1)}, u32[]{:S(2)}, u32[]{:S(2)}) %all-to-all-start.1) | async-done | bytes 442400 | tf_op jit(solution)/shard_map/all_to_all | solution.py:127
  307.3 1.4 copy.66
  308.7 0.8 fusion.121
  309.5 1.2 reshape.132
  310.7 2.0 reshape.134
  312.7 1.9 reshape.133
  314.6 2.2 fusion.128
  316.9 2.3 fusion.22
  319.1 1.0 copy.72
  320.1 0.9 convert_element_type.101
  321.0 0.9 copy.73
  321.9 0.8 copy.74
  322.8 6.9 all-to-all-start.2
  329.7 2.1 fusion.42
  331.8 2.6 fusion.23
  334.4 1.0 copy.84
  335.4 0.9 concatenate.15
  336.3 2.6 fusion.24
  338.9 1.0 copy.86
  339.9 0.9 concatenate.16
  340.8 2.3 fusion.25
  343.1 1.0 copy.88
  344.1 0.9 concatenate.17
  345.0 2.0 concatenate.18
  347.0 1.0 copy.89
  348.0 1.2 copy.90
  349.3 7.8 all-to-all-start.4
  357.1 4.9 reshape.149
  362.1 1.7 copy.199
  363.7 1.0 reshape.136
  364.8 1.6 convolution_convert_fusion
  366.4 4.0 all-to-all-done.4
  370.4 2.1 copy.198
  372.5 2.1 reshape.142
  374.6 3.1 fusion.6
  377.7 1.7 convolution_convert_fusion.1
  379.5 1.3 dynamic-slice
  380.7 1.3 dynamic-slice.2
  383.3 1.1 fusion.8
  386.1 1.6 fusion.26
  388.1 281.1 %all-reduce.9.cloned.1.call-done = (bf16[576,1152]{1,0:T(8,128)(2,1)}, bf16[576,1152]{1,0:T(8,128)(2,1)}) async-done(((bf16[576,1152]{1,0:T(8,128)(2,1)}, bf16[576,1152]{1,0:T(8,128)(2,1)}), (bf16[576,1152]{1,0:T(8,128)(2,1)}, bf16[576,1152]{1,0:T(8,128)(2,1)})) %all-reduce.9.cloned.1.call-update) | async-done | bytes 2654224
  669.2 1.6 constant_dynamic-slice_fusion
  670.8 1.5 fusion.27
  673.5 1.0 concatenate.19
  674.4 200.8 %all-reduce.11.cloned.1.call-done = (bf16[18,1152]{1,0:T(8,128)(2,1)}, bf16[18,1152]{1,0:T(8,128)(2,1)}) async-done(((bf16[18,1152]{1,0:T(8,128)(2,1)}, bf16[18,1152]{1,0:T(8,128)(2,1)}), (bf16[18,1152]{1,0:T(8,128)(2,1)}, bf16[18,1152]{1,0:T(8,128)(2,1)})) %all-reduce.11.cloned.1.call-update) | async-done | bytes 82960
  875.2 1.4 dynamic-slice_convert_fusion.1
  876.6 1.4 dynamic-slice_convert_fusion
  (62 shorter events, 5.4 us)
Async XLA Ops:
  7.2 25.2 %copy-start = (bf16[576,1152]{1,0:T(8,128)(2,1)S(1)}, bf16[576,1152]{1,0:T(8,128)(2,1)}, u32[]{:S(2)}) copy-start(bf16[576,1152]{1,0:T(8,128)(2,1)} %param.10) | copy-start | bytes 3981316
  10.6 18.8 %copy-start.11 = (bf16[2,64,1728]{2,1,0:T(8,128)(2,1)S(1)}, bf16[2,64,1728]{2,1,0:T(8,128)(2,1)}, u32[]{:S(2)}) copy-start(bf16[2,64,1728]{2,1,0:T(8,128)(2,1)} %param.7) | copy-start | bytes 1327108
  10.6 221.2 %all-to-all-start = ((bf16[16,1152,108]{1,2,0:T(8,128)(2,1)}), bf16[16,1152,108]{1,2,0:T(8,128)(2,1)}, u32[]{:S(2)}, u32[]{:S(2)}) async-start(bf16[16,1152,108]{1,2,0:T(8,128)(2,1)} %stack.2), calls=%async_computation | async-start | bytes 8257536 | tf_op jit(solution)/shard_map/all_to_all | solution.py:100
  28.6 328.5 %all-gather.3.cloned.1.call-start = ((), (), s32[]{:S(2)}) async-start(), calls=%async_computation.5 | async-start | bytes 4386816 | tf_op jit(solution)/shard_map/all_gather | solution.py:107
  29.8 1.7 copy-start.8
  30.0 1.9 copy-start.14
  30.3 1.6 copy-start.12
  31.5 1.0 copy-start.2
  32.4 206.6 %copy-start.4 = (bf16[128,576]{1,0:T(8,128)(2,1)}, bf16[128,576]{1,0:T(8,128)(2,1)S(1)}, u32[]{:S(2)}) copy-start(bf16[128,576]{1,0:T(8,128)(2,1)S(1)} %convert_element_type.94) | copy-start | bytes 442372
  32.4 206.5 %copy-start.1 = (bf16[576,1152]{1,0:T(8,128)(2,1)S(1)}, bf16[576,1152]{1,0:T(8,128)(2,1)}, u32[]{:S(2)}) copy-start(bf16[576,1152]{1,0:T(8,128)(2,1)} %param.8) | copy-start | bytes 3981316
  231.8 22.0 %all-to-all-start.3 = ((bf16[2,64,576]{2,0,1:T(2,128)(2,1)}), bf16[2,64,576]{2,0,1:T(2,128)(2,1)}, u32[]{:S(2)}, u32[]{:S(2)}) async-start(bf16[2,64,576]{2,0,1:T(2,128)(2,1)} %copy.77), calls=%async_computation.3 | async-start | bytes 327680 | tf_op jit(solution)/shard_map/all_to_all | solution.py:143
  253.8 53.5 %all-to-all-start.1 = ((bf16[2,64,1728]{2,0,1:T(2,128)(2,1)}), bf16[2,64,1728]{2,0,1:T(2,128)(2,1)}, u32[]{:S(2)}, u32[]{:S(2)}) async-start(bf16[2,64,1728]{2,0,1:T(2,128)(2,1)} %copy.65), calls=%async_computation.1 | async-start | bytes 917504 | tf_op jit(solution)/shard_map/all_to_all | solution.py:127
  310.7 6.1 copy-start.10
  322.8 9.0 %copy-start.16 = (bf16[8,16,8,72]{3,2,1,0:T(8,128)(2,1)S(1)}, bf16[8,16,8,72]{3,2,1,0:T(8,128)(2,1)}, u32[]{:S(2)}) copy-start(bf16[8,16,8,72]{3,2,1,0:T(8,128)(2,1)} %reshape.134) | copy-start | bytes 442372
  322.8 26.5 %all-to-all-start.2 = ((bf16[64,2,576]{2,1,0:T(2,128)(2,1)}), bf16[64,2,576]{2,1,0:T(2,128)(2,1)}, u32[]{:S(2)}, u32[]{:S(2)}) async-start(bf16[64,2,576]{2,1,0:T(2,128)(2,1)} %copy.74), calls=%async_computation.2 | async-start | bytes 327680 | tf_op jit(solution)/shard_map/all_to_all | solution.py:130
  349.3 21.1 %all-to-all-start.4 = ((bf16[64,2,1728]{2,1,0:T(2,128)(2,1)}), bf16[64,2,1728]{2,1,0:T(2,128)(2,1)}, u32[]{:S(2)}, u32[]{:S(2)}) async-start(bf16[64,2,1728]{2,1,0:T(2,128)(2,1)} %copy.90), calls=%async_computation.4 | async-start | bytes 917504 | tf_op jit(solution)/shard_map/all_to_all | solution.py:148
  357.0 312.1 %all-reduce.9.cloned.1.call-start = ((), (), s32[]{:S(2)}) async-start(), calls=%async_computation.6 | async-start | bytes 5308416
  364.8 7.7 copy-start.6
  374.6 3.1 copy-start.5
  377.7 6.7 copy-start.3
  379.4 3.9 copy-start.7
  379.4 495.8 %all-reduce.11.cloned.1.call-start = ((), (), s32[]{:S(2)}) async-start(), calls=%async_computation.7 | async-start | bytes 221184
  384.4 1.0 copy-start.9
  385.1 1.0 copy-start.15
  386.1 1.6 copy-start.13
Sparse Core Ops, SparseCore 0:
  32.5 273.7 all-gather.2
  379.5 289.5 all-reduce.8
  672.2 202.9 all-reduce.10
